TPU v7x, 256 devices: a whole 4x4x8 slice. The times are simulated.
256 devices in a mesh: tok: 16 (over y, x), col: 16 (over z, core).
Axes of the slice: x: 4, y: 4, z: 8, core: 2. Of those that a mesh axis runs over, the one named last changes fastest.
Arguments:
- activations: bfloat16 [32768, 8192], P('tok', 'col'), may hold values from -60 to 60, as said below
- weight: bfloat16 [8192, 8192], P('tok', 'col'), may hold values from -6 to 6
- keep_mask: int32 [8192, 8192], P('tok', 'col'), may hold values from 0 to 1
Outputs:
- new_weight: bfloat16 [8192, 8192], P('tok', 'col')
Inputs may be any that keep to these rules, and one draw needn't show every extreme that they name: activations of calibration tokens.
All inputs are finite; a program needn't handle non-finite values.
Results may differ from a plain program's by a relative error of at most 0.00115.
Values may be sent and summed in bfloat16 or wider, within the bound.
A program may use at most 64 MiB of HBM per device.

v0:
```python
import jax
import jax.numpy as jnp
from jax import lax
from jax.sharding import PartitionSpec as P

B = 1024
ITERS = 4


def split(x):
    high = lax.reduce_precision(x, exponent_bits=8, mantissa_bits=7)
    return (high.astype(jnp.bfloat16), (x - high).astype(jnp.bfloat16))


def mm(a, b, dims=(((1,), (0,)), ((), ()))):
    return lax.dot_general(a, b, dims, preferred_element_type=jnp.float32)


def per_device(activations, weight, keep_mask):
    n_col = lax.axis_size("col")
    n_tok = lax.axis_size("tok")
    tok_rows = activations.shape[0]
    panel_width = B // n_col
    total_count = tok_rows * n_tok
    pruned = jnp.where(
        keep_mask[:, :panel_width] == 0, weight[:, :panel_width], jnp.zeros((), jnp.bfloat16)
    )
    panel = lax.all_gather(activations[:, :panel_width], "col", axis=1, tiled=True)
    partial_panel = mm(activations, panel, (((0,), (0,)), ((), ())))
    pruned_panel = lax.all_gather(pruned, "col", axis=1, tiled=True)
    hessian_panel = lax.psum(partial_panel, "tok") / total_count
    block = lax.all_gather(hessian_panel[:panel_width], "col", axis=0, tiled=True)
    rows = lax.broadcasted_iota(jnp.int32, (B, B), 0)
    columns = lax.broadcasted_iota(jnp.int32, (B, B), 1)
    on_diagonal = rows == columns
    mean_diagonal = jnp.sum(jnp.where(on_diagonal, block, 0.0)) / B
    damped = block + jnp.where(on_diagonal, 0.01 * mean_diagonal, 0.0)
    scale = lax.rsqrt(jnp.sum(damped * damped))
    g = damped * scale
    y = pruned_panel.astype(jnp.float32)
    for sweep in range(ITERS):
        g_high = g.astype(jnp.bfloat16)
        y_high, y_low = split(y)
        y = 2.0 * y - (mm(y_high, g_high) + mm(y_low, g_high))
        if sweep < ITERS - 1:
            g = 2.0 * g - mm(g_high, g_high)
    y_high, y_low = split(y * scale)
    h_high, h_low = split(hessian_panel)
    nt = (((1,), (1,)), ((), ()))
    correction = mm(y_high, h_high, nt) + mm(y_low, h_high, nt) + mm(y_high, h_low, nt)
    kept = keep_mask.astype(jnp.float32)
    return (kept * (weight.astype(jnp.float32) - correction)).astype(jnp.bfloat16)


def solution(mesh):
    return jax.shard_map(
        per_device,
        mesh=mesh,
        in_specs=(P("tok", "col"), P("tok", "col"), P("tok", "col")),
        out_specs=P("tok", "col"),
        check_vma=False,
    )
```

profile of v0, /device:TPU:1, one launch (start us, length us, event | category | flops | bytes accessed | tf_op | source)
XLA Modules:
  0.0 284.6 jit_solution(3406045359667828655)
XLA Ops:
  6.5 0.0 all-gather.6.cloned.1.call-start
  6.5 1.2 slice.14
  7.8 0.9 copy.10
  8.7 0.0 all-gather.6.cloned.1.call-update
  8.7 0.0 all-reduce.2.cloned.1.call-start
  8.7 46.8 %all-gather.6.cloned.1.call-done = bf16[2048,1024]{0,1:T(8,128)(2,1)} async-done(((bf16[2048,64]{0,1:T(8,128)(2,1)}), bf16[2048,1024]{0,1:T(8,128)(2,1)}) %all-gather.6.cloned.1.call-update) | async-done | bytes 4194320 | tf_op jit(solution)/shard_map/all_gather | solution.py:28
  55.5 0.0 copy-done.4
  55.6 5.9 %fusion.29 = f32[512,1024]{1,0:T(8,128)} fusion(bf16[2048,512]{1,0:T(8,128)(2,1)S(1)} %copy-done.4, bf16[2048,1024]{0,1:T(8,128)(2,1)} %all-gather.6.cloned.1.call-done), kind=kOutput, calls=%fused_computation.50 | convolution fusion | flops 2147483648 | bytes 8388608 | tf_op jit(solution)/shard_map/dot_general | solution.py:16
  61.5 0.0 all-reduce.2.cloned.1.call-update
  61.5 0.0 all-gather.4.cloned.1.call-start
  61.5 0.8 slice-done.1
  62.4 0.1 copy.9
  62.5 0.0 slice-done
  62.5 0.1 copy.8
  62.6 0.6 compare_select_fusion
  63.2 0.0 all-gather.4.cloned.1.call-update
  63.3 0.0 all-gather.8.cloned.1.call-start
  63.3 95.8 %all-reduce.2.cloned.1.call-done = f32[512,1024]{1,0:T(8,128)} async-done(((f32[512,1024]{1,0:T(8,128)}), f32[512,1024]{1,0:T(8,128)}) %all-reduce.2.cloned.1.call-update) | async-done | bytes 2097168 | tf_op jit(solution)/shard_map/psum | solution.py:31
  159.1 1.8 broadcast_multiply_fusion
  160.9 0.7 slice.16
  161.6 0.0 all-gather.8.cloned.1.call-update
  161.6 39.0 %all-gather.4.cloned.1.call-done = bf16[512,1024]{0,1:T(8,128)(2,1)} async-done(((bf16[512,64]{0,1:T(8,128)(2,1)}), bf16[512,1024]{0,1:T(8,128)(2,1)}) %all-gather.4.cloned.1.call-update) | async-done | bytes 1048592 | tf_op jit(solution)/shard_map/all_gather | solution.py:30
  200.6 1.7 copy.6
  202.3 41.0 %all-gather.8.cloned.1.call-done = f32[1024,1024]{1,0:T(8,128)} async-done(((f32[64,1024]{1,0:T(8,128)}), f32[1024,1024]{1,0:T(8,128)}) %all-gather.8.cloned.1.call-update) | async-done | bytes 4194320 | tf_op jit(solution)/shard_map/all_gather | solution.py:32
  243.3 2.9 %select_reduce_fusion = f32[]{:T(128)} fusion(f32[1024,1024]{1,0:T(8,128)} %all-gather.8.cloned.1.call-done), kind=kLoop, calls=%fused_computation.5 | loop fusion | flops 3145727 | bytes 4194308 | tf_op jit(solution)/shard_map/reduce_sum | solution.py:36
  246.9 3.9 %multiply_reduce_fusion = f32[]{:T(128)} fusion(f32[1024,1024]{1,0:T(8,128)} %all-gather.8.cloned.1.call-done, f32[]{:T(128)S(6)} %mul_shard_map.3), kind=kLoop, calls=%fused_computation.3 | loop fusion | flops 5242879 | bytes 4194312 | tf_op jit(solution)/shard_map/reduce_sum | solution.py:38
  251.4 7.0 %multiply_subtract_fusion.1 = f32[1024,1024]{1,0:T(8,128)S(1)} fusion(f32[1024,1024]{1,0:T(8,128)} %all-gather.8.cloned.1.call-done, f32[]{:T(128)S(6)} %rsqrt.3, f32[]{:T(128)S(6)} %mul_shard_map.3), kind=kOutput, calls=%fused_computation.2 | convolution fusion | flops 2159017984 | bytes 8388616 | tf_op jit(solution)/shard_map/dot_general | solution.py:16
  258.5 0.0 copy-start.1
  258.5 2.3 multiply_subtract_fusion
  260.8 0.0 copy-done.1
  260.8 1.3 fusion.20
  262.1 1.4 fusion.6
  263.5 1.3 fusion.17
  264.8 1.3 add_subtract_fusion.1
  266.2 2.4 subtract_convert_fusion
  268.5 1.3 fusion.18
  269.8 1.6 add_subtract_fusion
  271.5 1.3 fusion.19
  272.7 0.0 copy-start
  272.7 1.4 subtract_multiply_fusion
  274.1 0.2 copy-done
  274.3 0.7 fusion.22
  275.1 0.0 copy-start.2
  275.1 0.0 copy-start.3
  275.1 0.7 convolution_add_fusion.1
  275.9 0.4 copy-done.2
  276.3 0.1 copy-done.3
  276.4 1.6 fusion.10
  (3 shorter events, 0.0 us)
Async XLA Ops:
  6.5 49.0 %copy-start.4 = (bf16[2048,512]{1,0:T(8,128)(2,1)S(1)}, bf16[2048,512]{1,0:T(8,128)(2,1)}, u32[]{:S(2)}) copy-start(bf16[2048,512]{1,0:T(8,128)(2,1)} %param.3) | copy-start | bytes 6291460
  6.5 49.0 %all-gather.6.cloned.1.call-start = ((), (), s32[]{:S(2)}) async-start(), calls=%async_computation.1 | async-start | bytes 4456448 | tf_op jit(solution)/shard_map/all_gather | solution.py:28
  8.7 150.4 %all-reduce.2.cloned.1.call-start = ((), (), s32[]{:S(2)}) async-start(), calls=%async_computation.2 | async-start | bytes 4194304 | tf_op jit(solution)/shard_map/psum | solution.py:31
  61.5 0.9 slice-start.1
  61.5 1.0 slice-start
  61.5 139.1 %all-gather.4.cloned.1.call-start = ((), (), s32[]{:S(2)}) async-start(), calls=%async_computation | async-start | bytes 1114112 | tf_op jit(solution)/shard_map/all_gather | solution.py:30
  63.3 180.0 %all-gather.8.cloned.1.call-start = ((), (), s32[]{:S(2)}) async-start(), calls=%async_computation.3 | async-start | bytes 4456448 | tf_op jit(solution)/shard_map/all_gather | solution.py:32
  258.5 2.4 copy-start.1
  272.7 1.6 copy-start
  275.1 1.2 copy-start.2
  275.1 1.3 copy-start.3
Sparse Core Ops, SparseCore 0:
  9.2 46.3 all-gather.5
  61.6 97.4 all-reduce.1
  161.1 39.5 all-gather.3
  202.4 40.7 all-gather.7
where the time goes:
time: 285 us
  waiting for transfers between devices  223 us (78%)
  matrix products  31.6 us (11%)
  between operations  14.6 us (5%)
  other arithmetic  9.21 us (3%)
  local copies, waits for them, and re-layouts  6.38 us (2%)
    psum x1, waiting for transfers between devices, per_device(): hessian_panel = lax.psum(partial_panel, 'tok') / total_count  95.8 us
    all_gather x1, waiting for transfers between devices, per_device(): lax.all_gather(activations[:, :panel_width], 'col', axis=1, tiled=True)  46.8 us
    all_gather x1, waiting for transfers between devices, per_device(): lax.all_gather(hessian_panel[:panel_width], 'col', axis=0, tiled=True)  41 us
    all_gather x1, waiting for transfers between devices, per_device(): pruned_panel = lax.all_gather(pruned, 'col', axis=1, tiled=True)  39 us
    dot_general x15, matrix products, mm(): return lax.dot_general(a, b, dims, preferred_element_type=jnp.float32)  31.6 us
  transfers between devices with their start and end apart: 4, of which 4 were waited for; matrix products, arithmetic and copies ran while one was open for 2% of the time, Pallas kernels for 0%

commit v1 on v0

--- a/solution.py
+++ b/solution.py
@@ -28,7 +28,7 @@
     panel = lax.all_gather(activations[:, :panel_width], "col", axis=1, tiled=True)
     partial_panel = mm(activations, panel, (((0,), (0,)), ((), ())))
     pruned_panel = lax.all_gather(pruned, "col", axis=1, tiled=True)
-    hessian_panel = lax.psum(partial_panel, "tok") / total_count
+    hessian_panel = jnp.sum(lax.all_gather(partial_panel, "tok"), axis=0) / total_count
     block = lax.all_gather(hessian_panel[:panel_width], "col", axis=0, tiled=True)
     rows = lax.broadcasted_iota(jnp.int32, (B, B), 0)
     columns = lax.broadcasted_iota(jnp.int32, (B, B), 1)

time: 285 us -> 387 us (1.36)
  waiting for transfers between devices: 223 us -> 314 us
  other arithmetic: 9.21 us -> 19.8 us
    all_gather x0 -> x1, waiting for transfers between devices: none -> 199 us  [per_device(): lax.all_gather(partial_panel, 'tok')]
    psum x1 -> x0, waiting for transfers between devices: 95.8 us -> none  [per_device(): hessian_panel = lax.psum(partial_panel, 'tok') / total_count]
    reduce_sum x0 -> x1, other arithmetic: none -> 12.1 us  [per_device(): jnp.sum(lax.all_gather(partial_panel, 'tok'), axis=0) / total_count]
    all_gather x1, waiting for transfers between devices: 39 us -> 27.6 us  [per_device(): pruned_panel = lax.all_gather(pruned, 'col', axis=1, tiled=True)]
  transfers between devices with their start and end apart: 4 -> 4, of which waited for: 4 -> 4; matrix products, arithmetic and copies ran while one was open for 2% -> 4% of each run, Pallas kernels for 0% -> 0%
where the time goes in v1:
time: 387 us; the launch traced here: 386 us
  waiting for transfers between devices  314 us (81%)
  matrix products  31.8 us (8%)
  other arithmetic  19.8 us (5%)
  between operations  14.6 us (4%)
  local copies, waits for them, and re-layouts  6.14 us (2%)
    all_gather x1, waiting for transfers between devices, per_device(): lax.all_gather(partial_panel, 'tok')  199 us
    all_gather x1, waiting for transfers between devices, per_device(): lax.all_gather(activations[:, :panel_width], 'col', axis=1, tiled=True)  46.8 us
    all_gather x1, waiting for transfers between devices, per_device(): lax.all_gather(hessian_panel[:panel_width], 'col', axis=0, tiled=True)  40.8 us
    dot_general x15, matrix products, mm(): return lax.dot_general(a, b, dims, preferred_element_type=jnp.float32)  31.8 us
    all_gather x1, waiting for transfers between devices, per_device(): pruned_panel = lax.all_gather(pruned, 'col', axis=1, tiled=True)  27.6 us
    reduce_sum x1, other arithmetic, per_device(): jnp.sum(lax.all_gather(partial_panel, 'tok'), axis=0) / total_count  12.1 us
  transfers between devices with their start and end apart: 4, of which 4 were waited for; matrix products, arithmetic and copies ran while one was open for 4% of the time, Pallas kernels for 0%

profile of v1, /device:TPU:1, one launch (start us, length us, event | category | flops | bytes accessed | tf_op | source)
XLA Modules:
  0.0 386.3 jit_solution(1877371268922955380)
XLA Ops:
  6.5 0.0 copy-start.3
  6.5 0.0 all-gather.8.cloned.1.call-start
  6.5 1.2 slice.14
  7.8 0.9 copy.10
  8.7 0.0 all-gather.8.cloned.1.call-update
  8.7 0.0 all-gather.12.cloned.1.call-start
  8.7 46.8 %all-gather.8.cloned.1.call-done = bf16[2048,1024]{0,1:T(8,128)(2,1)} async-done(((bf16[2048,64]{0,1:T(8,128)(2,1)}), bf16[2048,1024]{0,1:T(8,128)(2,1)}) %all-gather.8.cloned.1.call-update) | async-done | bytes 4194320 | tf_op jit(solution)/shard_map/all_gather | solution.py:28
  55.5 0.0 copy-done.3
  55.6 5.9 %fusion.29 = f32[512,1024]{1,0:T(8,128)} fusion(bf16[2048,512]{1,0:T(8,128)(2,1)S(1)} %copy-done.3, bf16[2048,1024]{0,1:T(8,128)(2,1)} %all-gather.8.cloned.1.call-done), kind=kOutput, calls=%fused_computation.50 | convolution fusion | flops 2147483648 | bytes 8388608 | tf_op jit(solution)/shard_map/dot_general | solution.py:16
  61.5 0.0 all-gather.12.cloned.1.call-update
  61.5 0.0 all-gather.6.cloned.1.call-start
  61.5 0.9 slice-done
  62.4 0.1 copy.8
  62.5 0.0 slice-done.1
  62.5 0.1 copy.9
  62.6 0.6 compare_select_fusion
  63.3 0.0 all-gather.6.cloned.1.call-update
  63.3 0.0 all-gather.10.cloned.1.call-start
  63.3 198.5 %all-gather.12.cloned.1.call-done = f32[8192,1024]{1,0:T(8,128)} async-done(((f32[512,1024]{1,0:T(8,128)}), f32[8192,1024]{1,0:T(8,128)}) %all-gather.12.cloned.1.call-update) | async-done | bytes 33554448 | tf_op jit(solution)/shard_map/all_gather | solution.py:31
  261.9 12.1 %reduce_sum.27 = f32[512,1024]{1,0:T(8,128)S(1)} reduce(f32[16,512,1024]{2,1,0:T(8,128)} %bitcast.5, f32[]{:T(128)} %constant.4.clone.1), dimensions={0}, to_apply=%region_0.1 | reduce | flops 7864320 | bytes 35651588 | tf_op jit(solution)/shard_map/reduce_sum | solution.py:31
  274.0 0.2 broadcast_multiply_fusion
  274.2 0.7 slice.16
  274.9 0.0 all-gather.10.cloned.1.call-update
  275.0 27.6 %all-gather.6.cloned.1.call-done = bf16[512,1024]{0,1:T(8,128)(2,1)} async-done(((bf16[512,64]{0,1:T(8,128)(2,1)}), bf16[512,1024]{0,1:T(8,128)(2,1)}) %all-gather.6.cloned.1.call-update) | async-done | bytes 1048592 | tf_op jit(solution)/shard_map/all_gather | solution.py:30
  302.5 1.7 copy.6
  304.2 40.8 %all-gather.10.cloned.1.call-done = f32[1024,1024]{1,0:T(8,128)} async-done(((f32[64,1024]{1,0:T(8,128)}), f32[1024,1024]{1,0:T(8,128)}) %all-gather.10.cloned.1.call-update) | async-done | bytes 4194320 | tf_op jit(solution)/shard_map/all_gather | solution.py:32
  345.0 2.9 select_reduce_fusion
  348.6 3.9 %multiply_reduce_fusion = f32[]{:T(128)} fusion(f32[1024,1024]{1,0:T(8,128)} %all-gather.10.cloned.1.call-done, f32[]{:T(128)S(6)} %mul_shard_map.3), kind=kLoop, calls=%fused_computation.3 | loop fusion | flops 5242879 | bytes 4194312 | tf_op jit(solution)/shard_map/reduce_sum | solution.py:38
  353.2 7.1 %multiply_subtract_fusion.1 = f32[1024,1024]{1,0:T(8,128)S(1)} fusion(f32[1024,1024]{1,0:T(8,128)} %all-gather.10.cloned.1.call-done, f32[]{:T(128)S(6)} %rsqrt.3, f32[]{:T(128)S(6)} %mul_shard_map.3), kind=kOutput, calls=%fused_computation.2 | convolution fusion | flops 2159017984 | bytes 8388616 | tf_op jit(solution)/shard_map/dot_general | solution.py:16
  360.3 0.0 copy-start
  360.3 2.3 multiply_subtract_fusion
  362.6 0.0 copy-done
  362.6 1.3 fusion.20
  364.0 1.4 fusion.6
  365.3 1.3 fusion.17
  366.6 1.3 add_subtract_fusion.1
  368.0 2.4 subtract_convert_fusion
  370.3 1.3 fusion.18
  371.6 1.6 add_subtract_fusion
  373.3 1.3 fusion.19
  374.5 1.4 subtract_multiply_fusion
  376.0 0.8 fusion.22
  376.7 0.0 copy-start.1
  376.7 0.0 copy-start.2
  376.8 0.8 convolution_add_fusion.1
  377.6 0.4 copy-done.1
  378.0 0.1 copy-done.2
  378.1 1.6 fusion.10
  (2 shorter events, 0.0 us)
Async XLA Ops:
  6.5 49.0 %copy-start.3 = (bf16[2048,512]{1,0:T(8,128)(2,1)S(1)}, bf16[2048,512]{1,0:T(8,128)(2,1)}, u32[]{:S(2)}) copy-start(bf16[2048,512]{1,0:T(8,128)(2,1)} %param.3) | copy-start | bytes 6291460
  6.5 49.0 %all-gather.8.cloned.1.call-start = ((), (), s32[]{:S(2)}) async-start(), calls=%async_computation.1 | async-start | bytes 4456448 | tf_op jit(solution)/shard_map/all_gather | solution.py:28
  8.7 253.2 %all-gather.12.cloned.1.call-start = ((), (), s32[]{:S(2)}) async-start(), calls=%async_computation.3 | async-start | bytes 35651584 | tf_op jit(solution)/shard_map/all_gather | solution.py:31
  61.5 0.9 slice-start
  61.5 1.1 slice-start.1
  61.5 241.0 %all-gather.6.cloned.1.call-start = ((), (), s32[]{:S(2)}) async-start(), calls=%async_computation | async-start | bytes 1114112 | tf_op jit(solution)/shard_map/all_gather | solution.py:30
  63.3 281.7 %all-gather.10.cloned.1.call-start = ((), (), s32[]{:S(2)}) async-start(), calls=%async_computation.2 | async-start | bytes 4456448 | tf_op jit(solution)/shard_map/all_gather | solution.py:32
  360.3 2.4 copy-start
  376.7 1.2 copy-start.1
  376.7 1.3 copy-start.2
Sparse Core Ops, SparseCore 0:
  9.2 46.3 all-gather.7
  61.6 200.2 all-gather.11
  263.7 38.7 all-gather.5
  304.2 40.7 all-gather.9
